TPU v7x, 32 devices: a whole 2x2x4 slice. The times are simulated.
32 devices in a mesh: pts: 4 (over y, x), lmk: 8 (over z, core).
Axes of the slice: x: 2, y: 2, z: 4, core: 2. Of those that a mesh axis runs over, the one named last changes fastest.
Arguments:
- points: float32 [16384, 384], P('pts'), may hold values from -8 to 8
- labels: int32 [16384], P('pts'), may hold values from 0 to 127
- landmarks: float32 [16384, 384], P('lmk'), may hold values from -8 to 8
- coefficients: float32 [16384, 128], P('lmk'), may hold values from -4 to 4
Outputs:
- gradient: float32 [16384, 128], P('lmk')
All inputs are finite; a program needn't handle non-finite values.
Results may differ from a plain program's by a relative error of at most 0.0003.
Values sent between devices are 32-bit elements; how exact they have to be, the bound alone decides.
A program may use at most 128 MiB of HBM per device.

v0:
```python
import jax
import jax.numpy as jnp
from jax import lax
from jax.sharding import PartitionSpec as P

LOSS_SCALE = 8192.0
RIDGE = 0.5


def residual_rows(logits, labels):
    classes = logits.shape[1]
    expo = jnp.exp(logits)
    onehot = (labels[:, None] == jnp.arange(classes, dtype=jnp.int32)[None, :]).astype(jnp.float32)
    return expo / jnp.sum(expo, axis=1, keepdims=True) - onehot


def per_device(points, labels, landmarks, coefficients):
    high = lax.Precision.HIGHEST
    feats = points.shape[1]
    pnorm = jnp.sum(points * points, axis=1)
    lnorm = jnp.sum(landmarks * landmarks, axis=1)
    cross = jnp.dot(points, landmarks.T, precision=high, preferred_element_type=jnp.float32)
    kernel = jnp.exp(-(pnorm[:, None] + lnorm[None, :] - 2.0 * cross) / feats)
    partial_logits = jnp.dot(
        kernel, coefficients, precision=high, preferred_element_type=jnp.float32
    )
    logits = lax.psum(partial_logits, "lmk")
    resid = residual_rows(logits, labels)
    local_terms = lax.dot_general(
        kernel, resid, (((0,), (0,)), ((), ())), precision=high, preferred_element_type=jnp.float32
    )
    summed = lax.psum(local_terms, "pts")
    total_points = labels.shape[0] * lax.axis_size("pts")
    return summed * (LOSS_SCALE / total_points) + RIDGE * coefficients


def solution(mesh):
    in_specs = (P("pts", None), P("pts"), P("lmk", None), P("lmk", None))
    out_specs = P("lmk", None)
    return jax.shard_map(
        per_device, mesh=mesh, in_specs=in_specs, out_specs=out_specs, check_vma=False
    )
```

profile of v0, /device:TPU:0, one launch (start us, length us, event | category | flops | bytes accessed | tf_op | source)
XLA Modules:
  0.0 299.8 jit_solution(14387722691670884355)
XLA Ops:
  6.5 0.0 copy-start
  6.5 0.0 all-reduce.3.cloned.1.call-start
  6.5 2.3 multiply_reduce_fusion.1
  8.9 3.4 %multiply_reduce_fusion = f32[4096]{0:T(1024)S(1)} fusion(f32[4096,384]{1,0:T(8,128)} %param.4), kind=kLoop, calls=%fused_computation.11 | loop fusion | flops 3141632 | bytes 6307840 | tf_op jit(solution)/shard_map/reduce_sum | solution.py:20
  12.3 58.6 %fusion.20 = f32[4096,2048]{1,0:T(8,128)} fusion(f32[4096,384]{1,0:T(8,128)} %param.4, f32[2048,384]{1,0:T(8,128)} %param.6), kind=kOutput, calls=%fused_computation.26 | convolution fusion | flops 38654705664 | bytes 42991616 | tf_op jit(solution)/shard_map/dot_general | solution.py:22
  70.9 0.0 copy-done
  70.9 0.0 copy-start.1
  70.9 35.0 %fusion.1 = f32[4096,128]{1,0:T(8,128)} fusion(f32[2048,128]{1,0:T(8,128)S(1)} %copy-done, f32[4096,2048]{1,0:T(8,128)} %fusion.20, f32[2048]{0:T(1024)S(1)} %multiply_reduce_fusion.1, f32[4096]{0:T(1024)S(1)} %multiply_reduce_fusion), kind=kOutput, calls=%fused_computation.2 | convolution fusion | flops 12926844928 | bytes 36724736 | tf_op jit(solution)/shard_map/dot_general | solution.py:24
  105.8 0.0 all-reduce.3.cloned.1.call-update
  105.8 0.0 all-reduce.5.cloned.1.call-start
  105.9 68.0 %all-reduce.3.cloned.1.call-done = f32[4096,128]{1,0:T(8,128)} async-done(((f32[4096,128]{1,0:T(8,128)}), f32[4096,128]{1,0:T(8,128)}) %all-reduce.3.cloned.1.call-update) | async-done | bytes 2097168 | tf_op jit(solution)/shard_map/psum | solution.py:27
  173.9 2.2 exponential_reduce_fusion
  176.1 0.0 copy-done.1
  176.1 62.3 %fusion = f32[2048,128]{1,0:T(8,128)} fusion(f32[4096,2048]{1,0:T(8,128)} %fusion.20, f32[2048]{0:T(1024)S(1)} %multiply_reduce_fusion.1, f32[4096]{0:T(1024)S(1)} %multiply_reduce_fusion, f32[4096,128]{1,0:T(8,128)} %all-reduce.3.cloned.1.call-done, s32[4096]{0:T(1024)S(1)} %copy-done.1, f32[4096]{0:T(1024)S(1)} %exponential_reduce_fusion), kind=kOutput, calls=%fused_computation.1 | convolution fusion | flops 12928942080 | bytes 36757504 | tf_op jit(solution)/shard_map/dot_general | solution.py:29
  238.4 0.0 all-reduce.5.cloned.1.call-update
  238.4 52.2 %all-reduce.5.cloned.1.call-done = f32[2048,128]{1,0:T(8,128)} async-done(((f32[2048,128]{1,0:T(8,128)}), f32[2048,128]{1,0:T(8,128)}) %all-reduce.5.cloned.1.call-update) | async-done | bytes 1048592 | tf_op jit(solution)/shard_map/psum | solution.py:32
  290.6 2.3 add_multiply_fusion
Async XLA Ops:
  6.5 64.3 %copy-start = (f32[2048,128]{1,0:T(8,128)S(1)}, f32[2048,128]{1,0:T(8,128)}, u32[]{:S(2)}) copy-start(f32[2048,128]{1,0:T(8,128)} %param.7) | copy-start | bytes 3145732
  6.5 167.4 %all-reduce.3.cloned.1.call-start = ((), (), s32[]{:S(2)}) async-start(), calls=%async_computation | async-start | bytes 4194304 | tf_op jit(solution)/shard_map/psum | solution.py:27
  70.9 105.3 %copy-start.1 = (s32[4096]{0:T(1024)S(1)}, s32[4096]{0:T(1024)}, u32[]{:S(2)}) copy-start(s32[4096]{0:T(1024)} %param.5) | copy-start | bytes 49156
  105.8 184.8 %all-reduce.5.cloned.1.call-start = ((), (), s32[]{:S(2)}) async-start(), calls=%async_computation.1 | async-start | bytes 2097152 | tf_op jit(solution)/shard_map/psum | solution.py:32
Sparse Core Ops, SparseCore 0:
  106.0 67.8 all-reduce.2
  238.5 52.0 all-reduce.4
where the time goes:
time: 300 us
  matrix products  156 us (52%)
  waiting for transfers between devices  120 us (40%)
  between operations  13.4 us (4%)
  other arithmetic  10.2 us (3%)
    psum x1, waiting for transfers between devices, per_device(): logits = lax.psum(partial_logits, 'lmk')  68 us
    dot_general x1, matrix products, per_device(): lax.dot_general(kernel, resid, (((0,), (0,)), ((), ())), precision=high,...  62.3 us
    dot_general x1, matrix products, per_device(): jnp.dot(points, landmarks.T, precision=high, preferred_element_type=jnp.f...  58.6 us
    psum x1, waiting for transfers between devices, per_device(): summed = lax.psum(local_terms, 'pts')  52.2 us
    dot_general x1, matrix products, per_device(): jnp.dot(kernel, coefficients, precision=high, preferred_element_type=jnp....  35 us
  transfers between devices with their start and end apart: 2, of which 2 were waited for; matrix products, arithmetic and copies ran while one was open for 0% of the time, Pallas kernels for 0%

commit v1 on v0

--- a/solution.py
+++ b/solution.py
@@ -29,7 +29,10 @@
     local_terms = lax.dot_general(
         kernel, resid, (((0,), (0,)), ((), ())), precision=high, preferred_element_type=jnp.float32
     )
-    summed = lax.psum(local_terms, "pts")
+    size, summed = (lax.axis_size("pts"), local_terms)
+    for reach in [1 << k for k in range(size.bit_length() - 1)]:
+        swap = [(i, i ^ reach) for i in range(size)]
+        summed = summed + lax.ppermute(summed, "pts", swap)
     total_points = labels.shape[0] * lax.axis_size("pts")
     return summed * (LOSS_SCALE / total_points) + RIDGE * coefficients
 

time: 300 us -> 292 us (0.973)
  waiting for transfers between devices: 120 us -> 111 us
  starting transfers between devices: 0.04 us -> 3.08 us
    psum x1 -> x0, waiting for transfers between devices: 52.2 us -> none  [per_device(): summed = lax.psum(local_terms, 'pts')]
    ppermute x0 -> x2, waiting for transfers between devices: none -> 43.1 us  [per_device(): summed = summed + lax.ppermute(summed, 'pts', swap)]
    ppermute x0 -> x2, starting transfers between devices: none -> 3.08 us  [per_device(): summed = summed + lax.ppermute(summed, 'pts', swap)]
  transfers between devices with their start and end apart: 2 -> 3, of which waited for: 2 -> 3; matrix products, arithmetic and copies ran while one was open for 0% -> 0% of each run, Pallas kernels for 0% -> 0%
where the time goes in v1:
time: 292 us
  matrix products  155 us (53%)
  waiting for transfers between devices  111 us (38%)
  between operations  13.4 us (5%)
  other arithmetic  9.23 us (3%)
  starting transfers between devices  3.08 us (1%)
    psum x1, waiting for transfers between devices, per_device(): logits = lax.psum(partial_logits, 'lmk')  68.1 us
    dot_general x1, matrix products, per_device(): lax.dot_general(kernel, resid, (((0,), (0,)), ((), ())), precision=high,...  61.3 us
    dot_general x1, matrix products, per_device(): jnp.dot(points, landmarks.T, precision=high, preferred_element_type=jnp.f...  58.6 us
    ppermute x2, waiting for transfers between devices, per_device(): summed = summed + lax.ppermute(summed, 'pts', swap)  43.1 us
    dot_general x1, matrix products, per_device(): jnp.dot(kernel, coefficients, precision=high, preferred_element_type=jnp....  35 us
  transfers between devices with their start and end apart: 3, of which 3 were waited for; matrix products, arithmetic and copies ran while one was open for 0% of the time, Pallas kernels for 0%

profile of v1, /device:TPU:0, one launch (start us, length us, event | category | flops | bytes accessed | tf_op | source)
XLA Modules:
  0.0 291.8 jit_solution(4223287921521084234)
XLA Ops:
  6.5 0.0 copy-start
  6.5 0.0 all-reduce.2.cloned.1.call-start
  6.5 2.3 multiply_reduce_fusion.1
  8.9 3.4 %multiply_reduce_fusion = f32[4096]{0:T(1024)S(1)} fusion(f32[4096,384]{1,0:T(8,128)} %param.4), kind=kLoop, calls=%fused_computation.11 | loop fusion | flops 3141632 | bytes 6307840 | tf_op jit(solution)/shard_map/reduce_sum | solution.py:20
  12.3 58.6 %fusion.20 = f32[4096,2048]{1,0:T(8,128)} fusion(f32[4096,384]{1,0:T(8,128)} %param.4, f32[2048,384]{1,0:T(8,128)} %param.6), kind=kOutput, calls=%fused_computation.26 | convolution fusion | flops 38654705664 | bytes 42991616 | tf_op jit(solution)/shard_map/dot_general | solution.py:22
  70.9 0.0 copy-done
  70.9 0.0 copy-start.1
  70.9 35.0 %fusion.1 = f32[4096,128]{1,0:T(8,128)} fusion(f32[2048,128]{1,0:T(8,128)S(1)} %copy-done, f32[4096,2048]{1,0:T(8,128)} %fusion.20, f32[2048]{0:T(1024)S(1)} %multiply_reduce_fusion.1, f32[4096]{0:T(1024)S(1)} %multiply_reduce_fusion), kind=kOutput, calls=%fused_computation.2 | convolution fusion | flops 12926844928 | bytes 36724736 | tf_op jit(solution)/shard_map/dot_general | solution.py:24
  105.8 0.0 all-reduce.2.cloned.1.call-update
  105.8 68.1 %all-reduce.2.cloned.1.call-done = f32[4096,128]{1,0:T(8,128)} async-done(((f32[4096,128]{1,0:T(8,128)}), f32[4096,128]{1,0:T(8,128)}) %all-reduce.2.cloned.1.call-update) | async-done | bytes 2097168 | tf_op jit(solution)/shard_map/psum | solution.py:27
  173.9 2.2 exponential_reduce_fusion
  176.1 0.0 copy-done.1
  176.1 61.3 %fusion = f32[2048,128]{1,0:T(8,128)S(1)} fusion(f32[4096,2048]{1,0:T(8,128)} %fusion.20, f32[2048]{0:T(1024)S(1)} %multiply_reduce_fusion.1, f32[4096]{0:T(1024)S(1)} %multiply_reduce_fusion, f32[4096,128]{1,0:T(8,128)} %all-reduce.2.cloned.1.call-done, s32[4096]{0:T(1024)S(1)} %copy-done.1, f32[4096]{0:T(1024)S(1)} %exponential_reduce_fusion), kind=kOutput, calls=%fused_computation.1 | convolution fusion | flops 12928942080 | bytes 36757504 | tf_op jit(solution)/shard_map/dot_general | solution.py:29
  237.4 1.5 collective-permute-start
  239.0 22.0 %collective-permute-done = f32[2048,128]{1,0:T(8,128)S(1)} collective-permute-done((f32[2048,128]{1,0:T(8,128)S(1)}, f32[2048,128]{1,0:T(8,128)S(1)}, u32[]{:S(2)}, u32[]{:S(2)}) %collective-permute-start) | collective-permute-done | bytes 1048608 | tf_op jit(solution)/shard_map/ppermute | solution.py:35
  261.0 0.1 add.28
  261.1 1.5 collective-permute-start.1
  262.6 21.1 %collective-permute-done.1 = f32[2048,128]{1,0:T(8,128)S(1)} collective-permute-done((f32[2048,128]{1,0:T(8,128)S(1)}, f32[2048,128]{1,0:T(8,128)S(1)}, u32[]{:S(2)}, u32[]{:S(2)}) %collective-permute-start.1) | collective-permute-done | bytes 1048608 | tf_op jit(solution)/shard_map/ppermute | solution.py:35
  283.7 1.2 add_multiply_fusion
Async XLA Ops:
  6.5 64.3 %copy-start = (f32[2048,128]{1,0:T(8,128)S(1)}, f32[2048,128]{1,0:T(8,128)}, u32[]{:S(2)}) copy-start(f32[2048,128]{1,0:T(8,128)} %param.7) | copy-start | bytes 3145732
  6.5 167.4 %all-reduce.2.cloned.1.call-start = ((), (), s32[]{:S(2)}) async-start(), calls=%async_computation | async-start | bytes 4194304 | tf_op jit(solution)/shard_map/psum | solution.py:27
  70.9 105.3 %copy-start.1 = (s32[4096]{0:T(1024)S(1)}, s32[4096]{0:T(1024)}, u32[]{:S(2)}) copy-start(s32[4096]{0:T(1024)} %param.5) | copy-start | bytes 49156
  237.4 23.5 %collective-permute-start = (f32[2048,128]{1,0:T(8,128)S(1)}, f32[2048,128]{1,0:T(8,128)S(1)}, u32[]{:S(2)}, u32[]{:S(2)}) collective-permute-start(f32[2048,128]{1,0:T(8,128)S(1)} %fusion), channel_id=1, source_target_pairs={{0,8},{8,0},{16,24},{24,16},{1,9},{9,1},{17,25},{25,17},{2,10},{10... | collective-permute-start | bytes 3145736 | tf_op jit(solution)/shard_map/ppermute | solution.py:35
  261.1 22.7 %collective-permute-start.1 = (f32[2048,128]{1,0:T(8,128)S(1)}, f32[2048,128]{1,0:T(8,128)S(1)}, u32[]{:S(2)}, u32[]{:S(2)}) collective-permute-start(f32[2048,128]{1,0:T(8,128)S(1)} %add.28), channel_id=1, source_target_pairs={{0,16},{8,24},{16,0},{24,8},{1,17},{9,25},{17,1},{25,9},{2,18},{10... | collective-permute-start | bytes 3145736 | tf_op jit(solution)/shard_map/ppermute | solution.py:35
Sparse Core Ops, SparseCore 0:
  106.0 67.8 all-reduce.1
